TPU v7x, 512 devices: a whole 4x4x16 slice. The times are simulated.
512 devices in a mesh: batch: 64 (over z_lo, y, core), space: 8 (over x, z_hi).
Axes of the slice: x: 4, y: 4, z: 16 (z_hi: 2, z_lo: 8; z = z_hi * 8 + z_lo), core: 2. Of those that a mesh axis runs over, the one named last changes fastest.
Arguments:
- acts: bfloat16 [64, 32, 64, 640], P('batch', 'space'), may hold values from -6 to 6
- conv_weight: bfloat16 [5760, 640], P('batch', 'space'), may hold values from -0.078125 to 0.078125
- conv_bias: float32 [640], replicated, may hold values from -4 to 4
- out_cotangent: bfloat16 [64, 32, 64, 640], P('batch', 'space'), may hold values from -6 to 6
- basis_in: bfloat16 [5760, 64], P('batch'), may hold values from -0.078125 to 0.078125
- basis_out: bfloat16 [640, 64], P('batch'), may hold values from -0.25 to 0.25
- query_ids: int32 [8], replicated, may hold values from 0 to 63
Outputs:
- activated: bfloat16 [64, 32, 64, 640], P('batch', 'space')
- basis_in_new: bfloat16 [5760, 64], P('batch')
- scores: float32 [8, 64], P(None, 'batch')
All inputs are finite; a program needn't handle non-finite values.
Results may differ from a plain program's by a relative error of at most 0.0031.
Values may be sent and summed in bfloat16 or wider, within the bound.
No kernel may reach another device: no remote copies, remote signals or barrier semaphores. Data moves between devices by JAX's collectives and lax.ppermute only.
A program may use at most 64 MiB of HBM per device.

v0:
```python
import math
import jax
import jax.numpy as jnp
from jax import lax
from jax.sharding import PartitionSpec as P

DAMPING = 0.1


def extended(value, sides, width):
    for axis, dim in sides:
        size, length = (lax.axis_size(axis), value.shape[dim])
        up = [(i, (i + 1) % size) for i in range(size - 1)]
        down = [(j, i) for i, j in up]
        last = lax.slice_in_dim(value, length - width, length, axis=dim)
        initial = lax.slice_in_dim(value, 0, width, axis=dim)
        before = lax.ppermute(last, axis, up)
        after = lax.ppermute(initial, axis, down)
        value = jnp.concatenate([before, value, after], axis=dim)
    return value


def add_columns(segment, operand):
    return jnp.dot(operand, segment, preferred_element_type=jnp.float32)


def add_with_norms(segment, operand):
    summed = add_columns(segment, operand)
    squares = jnp.sum(jnp.square(segment.astype(jnp.float32)), axis=0)
    return (summed, squares)


def contract_rows(left_side, right_side):
    return lax.dot_general(
        left_side, right_side, (((0,), (0,)), ((), ())), preferred_element_type=jnp.float32
    )


def per_device(acts, conv_weight, conv_bias, out_cotangent, basis_in, basis_out, query_ids):
    ex_local, band_rows, band_cols, channels = acts.shape
    padded = extended(acts, (("space", 1),), 1)
    padded = jnp.pad(padded, ((0, 0), (0, 0), (1, 1), (0, 0)))
    shifted = [
        padded[:, row_shift : row_shift + band_rows, col_shift : col_shift + band_cols, :]
        for row_shift in range(3)
        for col_shift in range(3)
    ]
    positions = ex_local * band_rows * band_cols
    patches = jnp.stack(shifted, axis=3).reshape(positions, 9 * channels)
    kernel_cols = lax.all_gather(conv_weight, "batch", axis=0, tiled=True)
    preact = jnp.dot(
        patches,
        lax.all_gather(kernel_cols, "space", axis=1, tiled=True),
        preferred_element_type=jnp.float32,
    )
    preact = preact + conv_bias
    sigmoid_pre = jax.nn.sigmoid(preact)
    activated = (preact * sigmoid_pre).astype(jnp.bfloat16).reshape(acts.shape)
    grad_pre = (
        out_cotangent.reshape(positions, channels).astype(jnp.float32)
        * sigmoid_pre
        * (1.0 + preact * (1.0 - sigmoid_pre))
    ).astype(jnp.bfloat16)
    basis_rank = basis_in.shape[1]
    probe_in = add_columns(lax.all_gather(basis_in, "batch", axis=0, tiled=True), patches).astype(
        jnp.bfloat16
    )
    probe_out = add_columns(
        lax.all_gather(basis_out, "batch", axis=0, tiled=True), grad_pre
    ).astype(jnp.bfloat16)
    term_in = contract_rows(patches, probe_in)
    term_out = contract_rows(grad_pre, probe_out)
    summed = lax.psum((term_in, term_out), "space")
    owned_in, owned_out = (
        lax.psum_scatter(summed[0], "batch", scatter_dimension=0, tiled=True),
        lax.psum_scatter(summed[1], "batch", scatter_dimension=0, tiled=True),
    )
    total_positions = positions * lax.axis_size("batch") * lax.axis_size("space")
    basis_in_new = (owned_in / total_positions).astype(jnp.bfloat16)
    basis_out_new = (owned_out / total_positions).astype(jnp.bfloat16)
    raw_in, square_in = add_with_norms(
        lax.all_gather(basis_in_new, "batch", axis=0, tiled=True), patches
    )
    raw_out, square_out = add_with_norms(
        lax.all_gather(basis_out_new, "batch", axis=0, tiled=True), grad_pre
    )
    scale_in = jnp.sqrt(square_in)
    scale_out = jnp.sqrt(square_out)
    feat_in = (
        (raw_in / scale_in)
        .astype(jnp.bfloat16)
        .reshape(ex_local, band_rows * band_cols, basis_rank)
    )
    feat_out = (
        (raw_out / scale_out)
        .astype(jnp.bfloat16)
        .reshape(ex_local, band_rows * band_cols, basis_rank)
    )
    height = band_rows * lax.axis_size("space")
    projected = (
        jnp.einsum("epi,epj->eij", feat_out, feat_in, preferred_element_type=jnp.float32) / height
    )
    projected = lax.psum(projected, "space")
    scaled = projected / (scale_out[:, None] * scale_in[None, :] + DAMPING)
    all_projs = lax.all_gather(projected, "batch", axis=0, tiled=True)
    queries = jnp.take(all_projs, query_ids, axis=0)
    scores = jnp.einsum("qij,eij->qe", queries, scaled, precision=lax.Precision.HIGHEST) / (
        basis_rank * math.sqrt(basis_rank)
    )
    return (activated, basis_in_new, scores)


def solution(mesh):
    return jax.shard_map(
        per_device,
        mesh=mesh,
        in_specs=(
            P("batch", "space", None, None),
            P("batch", "space"),
            P(),
            P("batch", "space", None, None),
            P("batch", None),
            P("batch", None),
            P(),
        ),
        out_specs=(P("batch", "space", None, None), P("batch", None), P(None, "batch")),
        check_vma=False,
    )
```

profile of v0, /device:TPU:1, one launch (start us, length us, event | category | flops | bytes accessed | tf_op | source)
XLA Modules:
  0.0 1847.2 jit_solution(3337683036946885710)
XLA Ops:
  7.2 0.0 all-gather.8.cloned.1.call-start
  7.2 132.7 %all-gather = bf16[64,90,80]{1,2,0:T(8,128)(2,1)S(1)} all-gather(bf16[1,90,80]{1,2,0:T(8,128)(2,1)} %bitcast.90), channel_id=1, replica_groups=mesh['batch'=64,'space'=8] {'batch'}, dimensions={0}, use_global_device_ids=true | all-gather | bytes 936000 | tf_op jit(solution)/shard_map/all_gather | solution.py:50
  140.0 0.3 copy.15
  140.3 2.8 reshape.103
  143.1 0.0 all-gather.8.cloned.1.call-update
  143.1 0.0 all-reduce.7.cloned.1.call-start
  143.2 8.0 collective-permute-start
  151.2 1.3 collective-permute-start.1
  152.5 167.6 %all-gather.1 = bf16[64,90,64]{1,2,0:T(8,128)(2,1)S(1)} all-gather(bf16[1,90,64]{1,2,0:T(8,128)(2,1)S(1)} %bitcast.91), channel_id=1, replica_groups=mesh['batch'=64,'space'=8] {'batch'}, dimensions={0}, use_global_device_ids=true | all-gather | bytes 748800 | tf_op jit(solution)/shard_map/all_gather | solution.py:65
  320.1 165.3 %all-gather.2 = bf16[64,10,64]{2,1,0:T(8,128)(2,1)S(1)} all-gather(bf16[1,10,64]{2,1,0:T(8,128)(2,1)S(1)} %bitcast.92), channel_id=1, replica_groups=mesh['batch'=64,'space'=8] {'batch'}, dimensions={0}, use_global_device_ids=true | all-gather | bytes 83200 | tf_op jit(solution)/shard_map/all_gather | solution.py:69
  485.4 0.1 reshape.107
  485.5 0.7 copy.16
  486.2 2.4 reshape.105
  488.6 0.6 copy-done.1
  489.2 0.2 fusion.16
  489.4 0.9 fusion.25
  490.4 0.1 fusion.23
  490.6 0.1 fusion.21
  490.8 0.1 fusion.17
  490.9 2.0 copy.14
  492.9 0.9 copy.22
  493.7 4.5 fusion.3
  498.3 6.4 fusion.11
  504.7 1.3 fusion.2
  506.0 0.0 all-reduce.7.cloned.1.call-update
  506.0 0.0 all-gather.10.cloned.1.call-start
  506.1 1.3 dynamic-slice
  508.6 821.8 %all-reduce.7.cloned.1.call-done = (f32[5760,64]{0,1:T(8,128)}, f32[640,64]{1,0:T(8,128)}) async-done(((f32[5760,64]{0,1:T(8,128)}, f32[640,64]{1,0:T(8,128)}), (f32[5760,64]{0,1:T(8,128)}, f32[640,64]{1,0:T(8,128)})) %all-reduce.7.cloned.1.call-update) | async-done | bytes 1638416
  1330.4 0.9 constant_dynamic-slice_fusion.1
  1331.3 0.7 constant_dynamic-slice_fusion
  1332.0 66.9 %all-reduce.4 = (f32[90,64]{0,1:T(8,128)S(1)}, f32[10,64]{1,0:T(8,128)S(1)}) all-reduce(f32[90,64]{0,1:T(8,128)S(1)} %constant_dynamic-slice_fusion.1, f32[10,64]{1,0:T(8,128)S(1)} %constant_dynamic-slice_fusion), channel_id=1, replica_groups=mesh['batch'=64,'space'=8] {'space'}, use_global_device_ids=true, to_apply=%region_0.1 | all-reduce | flops 6400 | bytes 51200 | tf_op jit(solution)/shard_map/psum | solution.py:73
  1398.9 130.7 %all-gather.4 = bf16[64,90,64]{1,2,0:T(8,128)(2,1)S(1)} all-gather(bf16[1,90,64]{1,2,0:T(8,128)(2,1)S(1)} %fusion.45), channel_id=1, replica_groups=mesh['batch'=64,'space'=8] {'batch'}, dimensions={0}, use_global_device_ids=true | all-gather | bytes 748800 | tf_op jit(solution)/shard_map/all_gather | solution.py:82
  1529.6 1.6 copy.17
  1531.2 3.1 reshape.111
  1534.4 1.4 multiply_reduce_fusion
  1535.8 114.8 %all-gather.3 = bf16[64,10,64]{2,1,0:T(8,128)(2,1)S(1)} all-gather(bf16[1,10,64]{2,1,0:T(8,128)(2,1)S(1)} %fusion.29), channel_id=1, replica_groups=mesh['batch'=64,'space'=8] {'batch'}, dimensions={0}, use_global_device_ids=true | all-gather | bytes 83200 | tf_op jit(solution)/shard_map/all_gather | solution.py:85
  1650.5 0.7 reshape.109
  1651.3 1.0 multiply_reduce_fusion.1
  1652.3 1.2 fusion.1
  1653.5 2.3 fusion.6
  1655.7 60.8 %psum.23 = f32[1,64,64]{2,1,0:T(8,128)} all-reduce(f32[1,64,64]{2,1,0:T(8,128)S(1)} %fusion.6), channel_id=1, replica_groups=mesh['batch'=64,'space'=8] {'space'}, use_global_device_ids=true, to_apply=%region_6.7 | all-reduce | flops 4096 | bytes 32768 | tf_op jit(solution)/shard_map/psum | solution.py:103
  1716.5 0.0 all-gather.10.cloned.1.call-update
  1716.6 0.6 multiply_convert_fusion.1
  1717.2 0.8 add_divide_fusion.1
  1718.1 119.1 %all-gather.10.cloned.1.call-done = f32[64,64,64]{2,1,0:T(8,128)} async-done(((f32[1,64,64]{2,1,0:T(8,128)}), f32[64,64,64]{2,1,0:T(8,128)}) %all-gather.10.cloned.1.call-update) | async-done | bytes 1048592 | tf_op jit(solution)/shard_map/all_gather | solution.py:105
  1837.2 2.2 gather_fusion
  1839.4 0.1 broadcast_select_fusion
  1839.5 1.2 fusion.8
  (31 shorter events, 0.3 us)
Async XLA Ops:
  7.2 491.1 %all-gather.8.cloned.1.call-start = ((), (), s32[]{:S(2)}) async-start(), calls=%async_computation | async-start | bytes 8294400 | tf_op jit(solution)/shard_map/all_gather | solution.py:53
  139.9 3.2 copy-start
  139.9 12.6 copy-start.4
  140.0 180.1 %copy-start.5 = (bf16[10,64]{1,0:T(8,128)(2,1)S(1)}, bf16[10,64]{1,0:T(8,128)(2,1)}, u32[]{:S(2)}) copy-start(bf16[10,64]{1,0:T(8,128)(2,1)} %param.12) | copy-start | bytes 3844
  143.1 1187.3 %all-reduce.7.cloned.1.call-start = ((), (), s32[]{:S(2)}) async-start(), calls=%async_computation.2 | async-start | bytes 3604480
  143.2 345.4 %collective-permute-start = (bf16[1,1,64,640]{3,2,1,0:T(8,128)(2,1)S(1)}, bf16[1,1,64,640]{3,2,1,0:T(8,128)(2,1)S(1)}, u32[]{:S(2)}, u32[]{:S(2)}) collective-permute-start(bf16[1,1,64,640]{3,2,1,0:T(8,128)(2,1)S(1)} %get-tuple-element.9), channel_id=1, source_target_pairs={{0,1},{1,2},{2,3},{3,4},{4,5},{5,6},{6,7},{8,9},{9,10},{10,11},{11... | collective-permute-start | bytes 245768 | tf_op jit(solution)/shard_map/ppermute | solution.py:17
  151.2 337.4 %collective-permute-start.1 = (bf16[1,1,64,640]{3,2,1,0:T(8,128)(2,1)S(1)}, bf16[1,1,64,640]{3,2,1,0:T(8,128)(2,1)S(1)}, u32[]{:S(2)}, u32[]{:S(2)}) collective-permute-start(bf16[1,1,64,640]{3,2,1,0:T(8,128)(2,1)S(1)} %get-tuple-element.10), channel_id=1, source_target_pairs={{1,0},{2,1},{3,2},{4,3},{5,4},{6,5},{7,6},{9,8},{10,9},{11,10},{12... | collective-permute-start | bytes 245768 | tf_op jit(solution)/shard_map/ppermute | solution.py:18
  488.6 0.6 copy-start.1
  493.7 4.6 copy-start.6
  506.0 1331.2 %all-gather.10.cloned.1.call-start = ((), (), s32[]{:S(2)}) async-start(), calls=%async_computation.1 | async-start | bytes 2129920 | tf_op jit(solution)/shard_map/all_gather | solution.py:105
  1398.9 136.8 %copy-start.2 = (f32[90,64]{0,1:T(8,128)}, f32[90,64]{0,1:T(8,128)S(1)}, u32[]{:S(2)}) copy-start(f32[90,64]{0,1:T(8,128)S(1)} %get-tuple-element.5) | copy-start | bytes 69124
  1534.4 182.2 %copy-start.7 = (s32[8]{0:T(128)S(1)}, s32[8]{0:T(128)}, u32[]{:S(2)}) copy-start(s32[8]{0:T(128)} %param.13) | copy-start | bytes 100
  1651.3 65.3 %copy-start.3 = (f32[90,64]{0,1:T(8,128)S(1)}, f32[90,64]{0,1:T(8,128)}, u32[]{:S(2)}) copy-start(f32[90,64]{0,1:T(8,128)} %copy-done.2) | copy-start | bytes 69124
Sparse Core Ops, SparseCore 0:
  143.2 265.6 all-gather.7
  506.1 824.2 all-reduce.6
  1716.7 120.4 all-gather.9
where the time goes:
time: 1850 us
  waiting for transfers between devices  941 us (51%)
  blocking collectives  839 us (45%)
  local copies, waits for them, and re-layouts  20.8 us (1%)
    unnamed x4, waiting for transfers between devices  822 us
    all_gather x1, blocking collectives, per_device(): lax.all_gather(basis_in, 'batch', axis=0, tiled=True)  168 us
    all_gather x1, blocking collectives, per_device(): lax.all_gather(basis_out, 'batch', axis=0, tiled=True)  165 us
    all_gather x1, blocking collectives, per_device(): kernel_cols = lax.all_gather(conv_weight, 'batch', axis=0, tiled=True)  133 us
    all_gather x1, blocking collectives, per_device(): lax.all_gather(basis_in_new, 'batch', axis=0, tiled=True)  131 us
    all_gather x1, waiting for transfers between devices, per_device(): all_projs = lax.all_gather(projected, 'batch', axis=0, tiled=True)  119 us
    all_gather x1, blocking collectives, per_device(): lax.all_gather(basis_out_new, 'batch', axis=0, tiled=True)  115 us
    psum x1, blocking collectives, per_device(): summed = lax.psum((term_in, term_out), 'space')  66.9 us
  transfers between devices with their start and end apart: 5, of which 2 were waited for; matrix products, arithmetic and copies ran while one was open for 1% of the time, Pallas kernels for 0%

commit v1 on v0

--- a/solution.py
+++ b/solution.py
@@ -3,8 +3,13 @@
 import jax.numpy as jnp
 from jax import lax
 from jax.sharding import PartitionSpec as P
+from jax.lax import all_to_all, axis_size
 
 DAMPING = 0.1
+
+
+def close_the_ways(x_part):
+    return jnp.concatenate(all_to_all(jnp.stack(axis_size("batch") * [x_part]), "batch", 0, 0), 0)
 
 
 def extended(value, sides, width):
@@ -62,9 +67,7 @@
         * (1.0 + preact * (1.0 - sigmoid_pre))
     ).astype(jnp.bfloat16)
     basis_rank = basis_in.shape[1]
-    probe_in = add_columns(lax.all_gather(basis_in, "batch", axis=0, tiled=True), patches).astype(
-        jnp.bfloat16
-    )
+    probe_in = add_columns(close_the_ways(basis_in), patches).astype(jnp.bfloat16)
     probe_out = add_columns(
         lax.all_gather(basis_out, "batch", axis=0, tiled=True), grad_pre
     ).astype(jnp.bfloat16)

time: 1850 us -> 1810 us (0.978)
  blocking collectives: 839 us -> 671 us
  waiting for transfers between devices: 941 us -> 1060 us
    all_gather x1 -> x0, blocking collectives: 168 us -> none  [per_device(): lax.all_gather(basis_in, 'batch', axis=0, tiled=True)]
    all_gather x1, waiting for transfers between devices: 0.01 us -> 93.8 us  [per_device(): lax.all_gather(kernel_cols, 'space', axis=1, tiled=True)]
    unnamed x4, waiting for transfers between devices: 822 us -> 849 us
  transfers between devices with their start and end apart: 5 -> 6, of which waited for: 2 -> 3; matrix products, arithmetic and copies ran while one was open for 1% -> 1% of each run, Pallas kernels for 0% -> 0%
where the time goes in v1:
time: 1810 us
  waiting for transfers between devices  1060 us (59%)
  blocking collectives  671 us (37%)
  local copies, waits for them, and re-layouts  24.6 us (1%)
    unnamed x4, waiting for transfers between devices  849 us
    all_gather x1, blocking collectives, per_device(): lax.all_gather(basis_out, 'batch', axis=0, tiled=True)  167 us
    all_gather x1, blocking collectives, per_device(): kernel_cols = lax.all_gather(conv_weight, 'batch', axis=0, tiled=True)  131 us
    all_gather x1, blocking collectives, per_device(): lax.all_gather(basis_in_new, 'batch', axis=0, tiled=True)  131 us
    all_gather x1, waiting for transfers between devices, per_device(): all_projs = lax.all_gather(projected, 'batch', axis=0, tiled=True)  119 us
    all_gather x1, blocking collectives, per_device(): lax.all_gather(basis_out_new, 'batch', axis=0, tiled=True)  115 us
    all_gather x1, waiting for transfers between devices, per_device(): lax.all_gather(kernel_cols, 'space', axis=1, tiled=True)  93.8 us
    psum x1, blocking collectives, per_device(): summed = lax.psum((term_in, term_out), 'space')  66.9 us
  transfers between devices with their start and end apart: 6, of which 3 were waited for; matrix products, arithmetic and copies ran while one was open for 1% of the time, Pallas kernels for 0%

profile of v1, /device:TPU:1, one launch (start us, length us, event | category | flops | bytes accessed | tf_op | source)
XLA Modules:
  0.0 1808.7 jit_solution(14759491890769303178)
XLA Ops:
  7.2 0.0 all-gather.7.cloned.1.call-start
  7.2 130.9 %all-gather = bf16[64,90,80]{1,2,0:T(8,128)(2,1)S(1)} all-gather(bf16[1,90,80]{1,2,0:T(8,128)(2,1)} %bitcast.89), channel_id=1, replica_groups=mesh['batch'=64,'space'=8] {'batch'}, dimensions={0}, use_global_device_ids=true | all-gather | bytes 936000 | tf_op jit(solution)/shard_map/all_gather | solution.py:55
  138.1 0.3 copy.15
  138.5 2.8 reshape.109
  141.2 0.0 all-gather.7.cloned.1.call-update
  141.2 1.3 stack.32
  142.6 5.1 all-to-all-start
  147.6 0.0 all-reduce.7.cloned.1.call-start
  147.7 7.9 collective-permute-start
  155.7 1.3 collective-permute-start.1
  157.0 167.4 %all-gather.1 = bf16[64,10,64]{2,1,0:T(8,128)(2,1)S(1)} all-gather(bf16[1,10,64]{2,1,0:T(8,128)(2,1)S(1)} %bitcast.90), channel_id=1, replica_groups=mesh['batch'=64,'space'=8] {'batch'}, dimensions={0}, use_global_device_ids=true | all-gather | bytes 83200 | tf_op jit(solution)/shard_map/all_gather | solution.py:72
  324.4 0.1 reshape.111
  324.5 0.2 fusion.16
  324.7 0.1 fusion.23
  324.9 0.1 fusion.21
  325.2 0.1 fusion.17
  325.3 2.0 copy.14
  327.3 0.9 copy.22
  328.1 3.0 copy.16
  331.1 3.2 reshape.96
  334.3 4.6 fusion.3
  338.8 93.8 %all-gather.7.cloned.1.call-done = bf16[5760,640]{0,1:T(8,128)(2,1)} async-done(((bf16[5760,80]{0,1:T(8,128)(2,1)}), bf16[5760,640]{0,1:T(8,128)(2,1)}) %all-gather.7.cloned.1.call-update) | async-done | bytes 7372816 | tf_op jit(solution)/shard_map/all_gather | solution.py:58
  432.7 6.4 fusion.11
  439.0 1.3 fusion.2
  440.4 0.0 all-reduce.7.cloned.1.call-update
  440.4 0.0 all-gather.9.cloned.1.call-start
  440.5 1.3 dynamic-slice
  443.0 848.9 %all-reduce.7.cloned.1.call-done = (f32[5760,64]{0,1:T(8,128)}, f32[640,64]{1,0:T(8,128)}) async-done(((f32[5760,64]{0,1:T(8,128)}, f32[640,64]{1,0:T(8,128)}), (f32[5760,64]{0,1:T(8,128)}, f32[640,64]{1,0:T(8,128)})) %all-reduce.7.cloned.1.call-update) | async-done | bytes 1638416
  1292.0 0.9 constant_dynamic-slice_fusion.1
  1292.9 0.7 constant_dynamic-slice_fusion
  1293.6 66.9 %all-reduce.4 = (f32[90,64]{0,1:T(8,128)S(1)}, f32[10,64]{1,0:T(8,128)S(1)}) all-reduce(f32[90,64]{0,1:T(8,128)S(1)} %constant_dynamic-slice_fusion.1, f32[10,64]{1,0:T(8,128)S(1)} %constant_dynamic-slice_fusion), channel_id=1, replica_groups=mesh['batch'=64,'space'=8] {'space'}, use_global_device_ids=true, to_apply=%region_0.1 | all-reduce | flops 6400 | bytes 51200 | tf_op jit(solution)/shard_map/psum | solution.py:76
  1360.5 130.6 %all-gather.3 = bf16[64,90,64]{1,2,0:T(8,128)(2,1)S(1)} all-gather(bf16[1,90,64]{1,2,0:T(8,128)(2,1)S(1)} %fusion.45), channel_id=1, replica_groups=mesh['batch'=64,'space'=8] {'batch'}, dimensions={0}, use_global_device_ids=true | all-gather | bytes 748800 | tf_op jit(solution)/shard_map/all_gather | solution.py:85
  1491.1 1.7 copy.17
  1492.7 3.1 reshape.115
  1495.8 1.4 multiply_reduce_fusion
  1497.3 114.8 %all-gather.2 = bf16[64,10,64]{2,1,0:T(8,128)(2,1)S(1)} all-gather(bf16[1,10,64]{2,1,0:T(8,128)(2,1)S(1)} %fusion.29), channel_id=1, replica_groups=mesh['batch'=64,'space'=8] {'batch'}, dimensions={0}, use_global_device_ids=true | all-gather | bytes 83200 | tf_op jit(solution)/shard_map/all_gather | solution.py:88
  1612.0 0.7 reshape.113
  1612.8 1.0 multiply_reduce_fusion.1
  1613.8 1.2 fusion.1
  1615.0 2.3 fusion.6
  1617.2 60.8 %psum.23 = f32[1,64,64]{2,1,0:T(8,128)} all-reduce(f32[1,64,64]{2,1,0:T(8,128)S(1)} %fusion.6), channel_id=1, replica_groups=mesh['batch'=64,'space'=8] {'space'}, use_global_device_ids=true, to_apply=%region_6.7 | all-reduce | flops 4096 | bytes 32768 | tf_op jit(solution)/shard_map/psum | solution.py:106
  1678.0 0.0 all-gather.9.cloned.1.call-update
  1678.1 0.6 multiply_convert_fusion.1
  1678.7 0.8 add_divide_fusion.1
  1679.6 119.1 %all-gather.9.cloned.1.call-done = f32[64,64,64]{2,1,0:T(8,128)} async-done(((f32[1,64,64]{2,1,0:T(8,128)}), f32[64,64,64]{2,1,0:T(8,128)}) %all-gather.9.cloned.1.call-update) | async-done | bytes 1048592 | tf_op jit(solution)/shard_map/all_gather | solution.py:108
  1798.7 2.2 gather_fusion
  1800.9 0.1 broadcast_select_fusion
  1801.0 1.2 fusion.8
  (31 shorter events, 0.3 us)
Async XLA Ops:
  7.2 425.5 %all-gather.7.cloned.1.call-start = ((), (), s32[]{:S(2)}) async-start(), calls=%async_computation.1 | async-start | bytes 8294400 | tf_op jit(solution)/shard_map/all_gather | solution.py:58
  138.1 3.2 copy-start.3
  138.4 9.3 copy-start
  138.4 18.5 %copy-start.4 = (bf16[10,64]{1,0:T(8,128)(2,1)S(1)}, bf16[10,64]{1,0:T(8,128)(2,1)}, u32[]{:S(2)}) copy-start(bf16[10,64]{1,0:T(8,128)(2,1)} %param.12) | copy-start | bytes 3844
  142.6 185.6 %all-to-all-start = ((bf16[64,90,64]{1,2,0:T(8,128)(2,1)}), bf16[64,90,64]{1,2,0:T(8,128)(2,1)}, u32[]{:S(2)}, u32[]{:S(2)}) async-start(bf16[64,90,64]{1,2,0:T(8,128)(2,1)} %stack.32), calls=%async_computation | async-start | bytes 2097152 | tf_op jit(solution)/shard_map/all_to_all | solution.py:12
  147.6 1144.3 %all-reduce.7.cloned.1.call-start = ((), (), s32[]{:S(2)}) async-start(), calls=%async_computation.3 | async-start | bytes 3604480
  147.7 176.7 %collective-permute-start = (bf16[1,1,64,640]{3,2,1,0:T(8,128)(2,1)S(1)}, bf16[1,1,64,640]{3,2,1,0:T(8,128)(2,1)S(1)}, u32[]{:S(2)}, u32[]{:S(2)}) collective-permute-start(bf16[1,1,64,640]{3,2,1,0:T(8,128)(2,1)S(1)} %get-tuple-element.9), channel_id=1, source_target_pairs={{0,1},{1,2},{2,3},{3,4},{4,5},{5,6},{6,7},{8,9},{9,10},{10,11},{11... | collective-permute-start | bytes 245768 | tf_op jit(solution)/shard_map/ppermute | solution.py:22
  155.7 168.8 %collective-permute-start.1 = (bf16[1,1,64,640]{3,2,1,0:T(8,128)(2,1)S(1)}, bf16[1,1,64,640]{3,2,1,0:T(8,128)(2,1)S(1)}, u32[]{:S(2)}, u32[]{:S(2)}) collective-permute-start(bf16[1,1,64,640]{3,2,1,0:T(8,128)(2,1)S(1)} %get-tuple-element.10), channel_id=1, source_target_pairs={{1,0},{2,1},{3,2},{4,3},{5,4},{6,5},{7,6},{9,8},{10,9},{11,10},{12... | collective-permute-start | bytes 245768 | tf_op jit(solution)/shard_map/ppermute | solution.py:23
  334.3 98.4 %copy-start.5 = (f32[640]{0:T(1024)S(1)}, f32[640]{0:T(1024)}, u32[]{:S(2)}) copy-start(f32[640]{0:T(1024)} %param.9) | copy-start | bytes 7684
  440.4 1358.3 %all-gather.9.cloned.1.call-start = ((), (), s32[]{:S(2)}) async-start(), calls=%async_computation.2 | async-start | bytes 2129920 | tf_op jit(solution)/shard_map/all_gather | solution.py:108
  1360.5 136.8 %copy-start.1 = (f32[90,64]{0,1:T(8,128)}, f32[90,64]{0,1:T(8,128)S(1)}, u32[]{:S(2)}) copy-start(f32[90,64]{0,1:T(8,128)S(1)} %get-tuple-element.5) | copy-start | bytes 69124
  1495.8 182.2 %copy-start.6 = (s32[8]{0:T(128)S(1)}, s32[8]{0:T(128)}, u32[]{:S(2)}) copy-start(s32[8]{0:T(128)} %param.13) | copy-start | bytes 100
  1612.8 65.3 %copy-start.2 = (f32[90,64]{0,1:T(8,128)S(1)}, f32[90,64]{0,1:T(8,128)}, u32[]{:S(2)}) copy-start(f32[90,64]{0,1:T(8,128)} %copy-done.1) | copy-start | bytes 69124
Sparse Core Ops, SparseCore 0:
  141.4 291.2 all-gather.6
  440.5 851.3 all-reduce.6
  1678.2 120.4 all-gather.8
